TPU v7x, 32 devices: a whole 2x2x4 slice. The times are simulated.
32 devices in a mesh: band: 2 (over x), gx: 16 (over z, y, core).
Axes of the slice: x: 2, y: 2, z: 4, core: 2. Of those that a mesh axis runs over, the one named last changes fastest.
Arguments:
- slc_tiles: bfloat16 [64, 2, 64, 2048], P('gx', None, 'band'), parts along dimension 2, may hold values from -64 to 64
- look_weight: float32 [64, 2048], P('band'), parts along dimension 0, may hold values from 0.05 to 1
- pair_list: int32 [192, 2], replicated, may hold values from 0 to 63, as said below
Outputs:
- corrected: float32 [64, 64, 2048], P(None, 'band', 'gx'), parts along dimension 1
There are 2 independent parts, one for each index of `band`. A program takes and returns all parts, laid end to end along the dimension named above; an argument that names none is the same for every part. Nothing has to cross between parts.
Inputs may be any that keep to these rules, and one draw needn't show every extreme that they name: `pair_list`: row p is a pair of date indices; with d = p // 12, the reference date lies in d * 4 to (d + 1) * 4 - 1 and the secondary date is 1 to 4 dates after it.
All inputs are finite; a program needn't handle non-finite values.
Results may differ from a plain program's by a relative error of at most 0.0071.
Values may be sent and summed in bfloat16 or wider, within the bound.
No kernel may reach another device: no remote copies, remote signals or barrier semaphores. Data moves between devices by JAX's collectives and lax.ppermute only.
A program may use at most 128 MiB of HBM per device.

v0:
```python
import jax
import jax.numpy as jnp
from jax import lax
from jax.sharding import PartitionSpec as P

LOOK = 9


def from_behind(block, axis, distance):
    devices = range(lax.axis_size(axis))
    route = [(i - distance, i) for i in devices if i - distance in devices]
    return lax.ppermute(block, axis, route)


def box_sum(values, col_count):
    rim_width = LOOK // 2
    row_count = values.shape[-2]
    padded = jnp.pad(values, [(0, 0)] * (values.ndim - 2) + [(rim_width, rim_width), (0, 0)])
    running = padded[..., 0:row_count, :]
    for offset in range(1, LOOK):
        running = running + padded[..., offset : offset + row_count, :]
    summed = running[..., 0:col_count]
    for offset in range(1, LOOK):
        summed = summed + running[..., offset : offset + col_count]
    return summed


def observe(first_tile, second_tile, weight, col_count):
    first_re = first_tile[..., 0, :, :].astype(jnp.float32)
    first_im = first_tile[..., 1, :, :].astype(jnp.float32)
    second_re = second_tile[..., 0, :, :].astype(jnp.float32)
    second_im = second_tile[..., 1, :, :].astype(jnp.float32)
    cross_re = weight * (first_re * second_re + first_im * second_im)
    cross_im = weight * (first_im * second_re - first_re * second_im)
    power_first = weight * (first_re * first_re + first_im * first_im)
    power_second = weight * (second_re * second_re + second_im * second_im)
    stacked = jnp.stack([cross_re, cross_im, power_first, power_second], axis=0)
    looked = box_sum(stacked, col_count)
    return (looked[1] * lax.rsqrt(looked[2] * looked[3] + 1e-06)).astype(jnp.bfloat16)


def solve_normal(normal_matrix, projected):
    factor = jnp.linalg.cholesky(normal_matrix)
    return jax.scipy.linalg.cho_solve((factor, True), projected)


def body(slc_tiles, look_weight, pair_list):
    rim_width = LOOK // 2
    devices = lax.axis_size("gx")
    position = lax.axis_index("gx")
    date_dev = slc_tiles.shape[0]
    row_count = slc_tiles.shape[2]
    col_total = slc_tiles.shape[3]
    strip_cols = col_total // devices
    pair_total = pair_list.shape[0]
    pair_dev = pair_total // devices
    date_total = date_dev * devices
    weight_pad = jnp.pad(look_weight, ((0, 0), (rim_width, rim_width)))
    following = from_behind(slc_tiles, "gx", -1)
    local_tiles = jnp.concatenate([slc_tiles, following], axis=0)
    local_tiles = jnp.pad(local_tiles, ((0, 0), (0, 0), (0, 0), (rim_width, rim_width)))
    own_pairs = (
        lax.dynamic_slice_in_dim(pair_list, position * pair_dev, pair_dev, 0) - position * date_dev
    )

    def one_pair(pair_row):
        return observe(local_tiles[pair_row[0]], local_tiles[pair_row[1]], weight_pad, col_total)

    observed = lax.map(one_pair, own_pairs)
    blocks = observed.reshape(pair_dev, row_count, devices, strip_cols)
    strips = lax.all_to_all(blocks, "gx", split_axis=2, concat_axis=0, tiled=True)
    strips = strips.reshape(pair_total, row_count * strip_cols)
    date_ids = lax.iota(jnp.int32, date_total)
    incidence = (
        (date_ids[:, None] == pair_list[None, :, 0]).astype(jnp.float32)
        - (date_ids[:, None] == pair_list[None, :, 1]).astype(jnp.float32)
    ).astype(jnp.bfloat16)
    normal_matrix = jnp.dot(incidence, incidence.T, preferred_element_type=jnp.float32) + jnp.eye(
        date_total, dtype=jnp.float32
    )
    projected = jnp.dot(incidence, strips, preferred_element_type=jnp.float32)
    series = solve_normal(normal_matrix, projected).reshape(date_total, row_count, strip_cols)
    column_ids = position * strip_cols + lax.iota(jnp.int32, strip_cols)
    columns = (2.0 * column_ids.astype(jnp.float32) + 1.0) / col_total - 1.0
    all_cols = (2.0 * lax.iota(jnp.int32, col_total).astype(jnp.float32) + 1.0) / col_total - 1.0
    square_sum = jnp.sum(all_cols * all_cols)
    partial_mean = jnp.sum(series, axis=(1, 2))
    partial_slope = jnp.sum(series * columns, axis=(1, 2))
    totals = lax.psum((partial_mean, partial_slope), "gx")
    date_mean = totals[0] / (row_count * col_total)
    date_slope = totals[1] / (row_count * square_sum)
    return series - date_mean[:, None, None] - date_slope[:, None, None] * columns


def solution(mesh):
    return jax.shard_map(
        body,
        mesh=mesh,
        in_specs=(P("gx", None, "band", None), P("band", None), P()),
        out_specs=P(None, "band", "gx"),
        check_vma=False,
    )
```

profile of v0, /device:TPU:0, one launch (start us, length us, event | category | flops | bytes accessed | tf_op | source)
XLA Modules:
  0.0 213.2 jit_solution(9840836476358481530)
XLA Ops:
  0.0 1.3 collective-permute-start
  1.3 1.1 pad.15
  2.4 1.3 dynamic-slice_subtract_fusion
  3.7 1.0 collective-permute-done
  4.8 2.6 %fusion.28 = bf16[8,2,32,2056]{3,2,1,0:T(8,128)(2,1)S(1)} fusion(bf16[4,2,32,2048]{3,2,1,0:T(8,128)(2,1)S(1)} %collective-permute-done, bf16[4,2,32,2048]{3,2,1,0:T(8,128)(2,1)} %param.5), kind=kLoop, calls=%fused_computation.57 | loop fusion | flops 9474048 | bytes 4202496 | tf_op jit(solution)/shard_map/concatenate | solution.py:60
  7.3 108.7 %while.12 = (s32[]{:T(128)}, bf16[12,32,2048]{2,1,0:T(8,128)(2,1)}, f32[32,2056]{1,0:T(8,128)S(1)}, s32[12,2]{0,1:T(2,128)}, bf16[8,2,32,2056]{3,2,1,0:T(8,128)(...) while((s32[]{:T(128)}, bf16[12,32,2048]{2,1,0:T(8,128)(2,1)}, f32[32,2056]{1,0:T(8,128)S(1)}, ...), condition=%wide.region_3.4_spmd, body=%wide.region_2.3_spmd.sunk | while | flops 6569993 | bytes 17456360 | solution.py:69
  7.3 0.8 constant_dynamic-slice_fusion.2
  12.6 0.8 fusion.58
  13.5 2.2 %slice_add_fusion.9 = f32[4,32,2048]{2,1,0:T(8,128)S(1)} fusion(f32[4,32,2056]{2,1,0:T(8,128)S(1)} %fusion.58), kind=kLoop, calls=%fused_computation.17.clone.1 | loop fusion | flops 2097152 | bytes 10485760 | tf_op jit(solution)/shard_map/while/body/eval_jaxpr/add | solution.py:24
  16.4 0.7 constant_dynamic-slice_fusion.2
  21.7 0.8 fusion.58
  22.5 2.2 %slice_add_fusion.9 = f32[4,32,2048]{2,1,0:T(8,128)S(1)} fusion(f32[4,32,2056]{2,1,0:T(8,128)S(1)} %fusion.58), kind=kLoop, calls=%fused_computation.17.clone.1 | loop fusion | flops 2097152 | bytes 10485760 | tf_op jit(solution)/shard_map/while/body/eval_jaxpr/add | solution.py:24
  25.4 0.7 constant_dynamic-slice_fusion.2
  30.7 0.8 fusion.58
  31.6 2.2 %slice_add_fusion.9 = f32[4,32,2048]{2,1,0:T(8,128)S(1)} fusion(f32[4,32,2056]{2,1,0:T(8,128)S(1)} %fusion.58), kind=kLoop, calls=%fused_computation.17.clone.1 | loop fusion | flops 2097152 | bytes 10485760 | tf_op jit(solution)/shard_map/while/body/eval_jaxpr/add | solution.py:24
  34.5 0.7 constant_dynamic-slice_fusion.2
  39.8 0.8 fusion.58
  40.6 2.2 %slice_add_fusion.9 = f32[4,32,2048]{2,1,0:T(8,128)S(1)} fusion(f32[4,32,2056]{2,1,0:T(8,128)S(1)} %fusion.58), kind=kLoop, calls=%fused_computation.17.clone.1 | loop fusion | flops 2097152 | bytes 10485760 | tf_op jit(solution)/shard_map/while/body/eval_jaxpr/add | solution.py:24
  43.6 0.7 constant_dynamic-slice_fusion.2
  48.9 0.8 fusion.58
  49.7 2.2 %slice_add_fusion.9 = f32[4,32,2048]{2,1,0:T(8,128)S(1)} fusion(f32[4,32,2056]{2,1,0:T(8,128)S(1)} %fusion.58), kind=kLoop, calls=%fused_computation.17.clone.1 | loop fusion | flops 2097152 | bytes 10485760 | tf_op jit(solution)/shard_map/while/body/eval_jaxpr/add | solution.py:24
  57.9 0.8 fusion.58
  58.7 2.2 %slice_add_fusion.9 = f32[4,32,2048]{2,1,0:T(8,128)S(1)} fusion(f32[4,32,2056]{2,1,0:T(8,128)S(1)} %fusion.58), kind=kLoop, calls=%fused_computation.17.clone.1 | loop fusion | flops 2097152 | bytes 10485760 | tf_op jit(solution)/shard_map/while/body/eval_jaxpr/add | solution.py:24
  61.7 0.7 constant_dynamic-slice_fusion.2
  67.0 0.8 fusion.58
  67.8 2.2 %slice_add_fusion.9 = f32[4,32,2048]{2,1,0:T(8,128)S(1)} fusion(f32[4,32,2056]{2,1,0:T(8,128)S(1)} %fusion.58), kind=kLoop, calls=%fused_computation.17.clone.1 | loop fusion | flops 2097152 | bytes 10485760 | tf_op jit(solution)/shard_map/while/body/eval_jaxpr/add | solution.py:24
  70.7 0.7 constant_dynamic-slice_fusion.2
  76.0 0.8 fusion.58
  76.8 2.2 %slice_add_fusion.9 = f32[4,32,2048]{2,1,0:T(8,128)S(1)} fusion(f32[4,32,2056]{2,1,0:T(8,128)S(1)} %fusion.58), kind=kLoop, calls=%fused_computation.17.clone.1 | loop fusion | flops 2097152 | bytes 10485760 | tf_op jit(solution)/shard_map/while/body/eval_jaxpr/add | solution.py:24
  79.8 0.7 constant_dynamic-slice_fusion.2
  85.1 0.8 fusion.58
  85.9 2.2 %slice_add_fusion.9 = f32[4,32,2048]{2,1,0:T(8,128)S(1)} fusion(f32[4,32,2056]{2,1,0:T(8,128)S(1)} %fusion.58), kind=kLoop, calls=%fused_computation.17.clone.1 | loop fusion | flops 2097152 | bytes 10485760 | tf_op jit(solution)/shard_map/while/body/eval_jaxpr/add | solution.py:24
  94.1 0.8 fusion.58
  95.0 2.2 %slice_add_fusion.9 = f32[4,32,2048]{2,1,0:T(8,128)S(1)} fusion(f32[4,32,2056]{2,1,0:T(8,128)S(1)} %fusion.58), kind=kLoop, calls=%fused_computation.17.clone.1 | loop fusion | flops 2097152 | bytes 10485760 | tf_op jit(solution)/shard_map/while/body/eval_jaxpr/add | solution.py:24
  103.2 0.8 fusion.58
  104.0 2.2 %slice_add_fusion.9 = f32[4,32,2048]{2,1,0:T(8,128)S(1)} fusion(f32[4,32,2056]{2,1,0:T(8,128)S(1)} %fusion.58), kind=kLoop, calls=%fused_computation.17.clone.1 | loop fusion | flops 2097152 | bytes 10485760 | tf_op jit(solution)/shard_map/while/body/eval_jaxpr/add | solution.py:24
  112.3 0.8 fusion.58
  113.1 2.2 %slice_add_fusion.9 = f32[4,32,2048]{2,1,0:T(8,128)S(1)} fusion(f32[4,32,2056]{2,1,0:T(8,128)S(1)} %fusion.58), kind=kLoop, calls=%fused_computation.17.clone.1 | loop fusion | flops 2097152 | bytes 10485760 | tf_op jit(solution)/shard_map/while/body/eval_jaxpr/add | solution.py:24
  116.0 3.0 %copy_bitcast_fusion = bf16[12,32,16,128]{3,1,0,2:T(8,128)(2,1)} fusion(bf16[12,32,2048]{2,1,0:T(8,128)(2,1)} %get-tuple-element.70), kind=kLoop, calls=%fused_computation.62 | loop fusion | bytes 3145728 | tf_op jit(solution)/shard_map/reshape | solution.py:70
  119.0 18.4 %all-to-all-start = ((bf16[12,32,16,128]{3,1,0,2:T(8,128)(2,1)}), bf16[12,32,16,128]{3,1,0,2:T(8,128)(2,1)S(1)}, u32[]{:S(2)}, u32[]{:S(2)}) async-start(bf16[12,32,16,128]{3,1,0,2:T(8,128)(2,1)} %copy_bitcast_fusion), calls=%async_computation | async-start | bytes 3145728 | tf_op jit(solution)/shard_map/all_to_all | solution.py:71
  137.7 5.8 %cholesky.17 = f32[64,64]{1,0:T(8,128)S(1)} custom-call(f32[64,64]{1,0:T(8,128)S(1)} %fusion.41), custom_call_target="Cholesky" | custom-call | tf_op jit(solution)/shard_map/jit(cholesky)/cholesky | solution.py:43
  144.9 4.9 %custom-call.10 = f32[1,64,64]{1,2,0:T(8,128)S(1)} custom-call(f32[1,64,64]{2,1,0:T(8,128)S(1)} %fusion.34), custom_call_target="InvertDiagBlocksLowerTriangular" | custom-call | tf_op jit(solution)/shard_map/jit(_cho_solve)/triangular_solve | solution.py:44
  151.1 18.2 %all-to-all-done = bf16[12,32,16,128]{3,1,0,2:T(8,128)(2,1)S(1)} async-done(((bf16[12,32,16,128]{3,1,0,2:T(8,128)(2,1)}), bf16[12,32,16,128]{3,1,0,2:T(8,128)(2,1)S(1)}, u32[]{:S(2)}, u32[]{:S(2)}) %all-to-all-start) | async-done | bytes 1572896 | tf_op jit(solution)/shard_map/all_to_all | solution.py:71
  169.3 1.2 fusion.29
  170.5 2.5 %fusion.38 = f32[32,128,64]{1,2,0:T(8,128)S(1)} fusion(f32[32,128,64]{2,1,0:T(8,128)S(1)} %fusion.29, f32[1,64,64]{1,2,0:T(8,128)S(1)} %custom-call.10), kind=kOutput, calls=%fused_computation.74 | convolution fusion | flops 201326592 | bytes 2113536 | tf_op jit(solution)/shard_map/jit(_cho_solve)/triangular_solve | solution.py:44
  173.0 1.2 fusion.46
  174.2 37.2 %all-reduce.3 = (f32[64]{0:T(128)S(1)}, f32[64]{0:T(128)S(1)}) all-reduce(f32[64]{0:T(128)S(1)} %get-tuple-element.72, f32[64]{0:T(128)S(1)} %get-tuple-element.71), channel_id=1, replica_groups=mesh['band'=2,'gx'=16] {'gx'}, use_global_device_ids=true, to_apply=%region_7.8 | all-reduce | flops 128 | bytes 1024 | tf_op jit(solution)/shard_map/psum | solution.py:89
  211.7 1.6 copy.8
  (67 shorter events, 23.7 us)
Async XLA Ops:
  0.0 4.8 %collective-permute-start = (bf16[4,2,32,2048]{3,2,1,0:T(8,128)(2,1)}, bf16[4,2,32,2048]{3,2,1,0:T(8,128)(2,1)S(1)}, u32[]{:S(2)}, u32[]{:S(2)}) collective-permute-start(bf16[4,2,32,2048]{3,2,1,0:T(8,128)(2,1)} %param.5), channel_id=1, source_target_pairs={{1,0},{2,1},{3,2},{4,3},{5,4},{6,5},{7,6},{8,7},{9,8},{10,9},{11,1... | collective-permute-start | bytes 3145736 | tf_op jit(solution)/shard_map/ppermute | solution.py:12
  119.0 18.4 %copy-start = (s32[192,2]{0,1:T(2,128)S(1)}, s32[192,2]{0,1:T(2,128)}, u32[]{:S(2)}) copy-start(s32[192,2]{0,1:T(2,128)} %param.7) | copy-start | bytes 4612
  119.0 50.3 %all-to-all-start = ((bf16[12,32,16,128]{3,1,0,2:T(8,128)(2,1)}), bf16[12,32,16,128]{3,1,0,2:T(8,128)(2,1)S(1)}, u32[]{:S(2)}, u32[]{:S(2)}) async-start(bf16[12,32,16,128]{3,1,0,2:T(8,128)(2,1)} %copy_bitcast_fusion), calls=%async_computation | async-start | bytes 3145728 | tf_op jit(solution)/shard_map/all_to_all | solution.py:71
where the time goes:
time: 214 us; the launch traced here: 213 us
  other arithmetic  65.1 us (30%)
  loops' own time  45 us (21%)
  blocking collectives  37.2 us (17%)
  local copies, waits for them, and re-layouts  21.2 us (10%)
  starting transfers between devices  19.7 us (9%)
  waiting for transfers between devices  19.2 us (9%)
  matrix products  5.02 us (2%)
    another operation x1, loops' own time, body(): observed = lax.map(one_pair, own_pairs)  45 us
    psum x1, blocking collectives, body(): totals = lax.psum((partial_mean, partial_slope), 'gx')  37.2 us
    add x12, other arithmetic, box_sum(): summed = summed + running[..., offset:offset + col_count]  26.7 us
    all_to_all x1, starting transfers between devices, body(): lax.all_to_all(blocks, 'gx', split_axis=2, concat_axis=0, tiled=True)  18.4 us
    all_to_all x1, waiting for transfers between devices, body(): lax.all_to_all(blocks, 'gx', split_axis=2, concat_axis=0, tiled=True)  18.2 us
    add x12, other arithmetic, box_sum(): running = running + padded[..., offset:offset + row_count, :]  9.79 us
    dynamic_slice x12, local copies, waits for them, and re-layouts, body(): observed = lax.map(one_pair, own_pairs)  9 us
    dynamic_update_slice x12, other arithmetic, body(): observed = lax.map(one_pair, own_pairs)  8.45 us
  transfers between devices with their start and end apart: 2, of which 2 were waited for; matrix products, arithmetic and copies ran while one was open for 7% of the time, Pallas kernels for 0%

commit v1 on v0

--- a/solution.py
+++ b/solution.py
@@ -68,7 +68,10 @@
 
     observed = lax.map(one_pair, own_pairs)
     blocks = observed.reshape(pair_dev, row_count, devices, strip_cols)
-    strips = lax.all_to_all(blocks, "gx", split_axis=2, concat_axis=0, tiled=True)
+    strips = jnp.concatenate(
+        lax.all_to_all(jnp.stack(jnp.split(blocks, lax.axis_size("gx"), axis=2)), "gx", 0, 0),
+        axis=0,
+    )
     strips = strips.reshape(pair_total, row_count * strip_cols)
     date_ids = lax.iota(jnp.int32, date_total)
     incidence = (

time: 214 us -> 225 us (1.051)
  local copies, waits for them, and re-layouts: 21.2 us -> 34 us
    unnamed x2 -> x18, local copies, waits for them, and re-layouts: 0.01 us -> 11.5 us
    split x0 -> x1, local copies, waits for them, and re-layouts: none -> 3.6 us  [body(): jnp.split(blocks, lax.axis_size('gx'), axis=2)]
    reshape x1 -> x0, local copies, waits for them, and re-layouts: 2.96 us -> none  [body(): blocks = observed.reshape(pair_dev, row_count, devices, strip_cols)]
where the time goes in v1:
time: 225 us; the launch traced here: 224 us
  other arithmetic  65.1 us (29%)
  loops' own time  45 us (20%)
  blocking collectives  37.2 us (17%)
  local copies, waits for them, and re-layouts  34 us (15%)
  starting transfers between devices  19.7 us (9%)
  waiting for transfers between devices  19.2 us (9%)
  matrix products  2.98 us (1%)
    another operation x1, loops' own time, body(): observed = lax.map(one_pair, own_pairs)  45 us
    psum x1, blocking collectives, body(): totals = lax.psum((partial_mean, partial_slope), 'gx')  37.2 us
    add x12, other arithmetic, box_sum(): summed = summed + running[..., offset:offset + col_count]  26.7 us
    all_to_all x1, starting transfers between devices, body(): lax.all_to_all(jnp.stack(jnp.split(blocks, lax.axis_size('gx'), axis=2)),...  18.4 us
    all_to_all x1, waiting for transfers between devices, body(): lax.all_to_all(jnp.stack(jnp.split(blocks, lax.axis_size('gx'), axis=2)),...  18.2 us
    unnamed x18, local copies, waits for them, and re-layouts  11.5 us
    add x12, other arithmetic, box_sum(): running = running + padded[..., offset:offset + row_count, :]  9.79 us
    dynamic_slice x12, local copies, waits for them, and re-layouts, body(): observed = lax.map(one_pair, own_pairs)  9 us
  transfers between devices with their start and end apart: 2, of which 2 were waited for; matrix products, arithmetic and copies ran while one was open for 7% of the time, Pallas kernels for 0%

profile of v1, /device:TPU:0, one launch (start us, length us, event | category | flops | bytes accessed | tf_op | source)
XLA Modules:
  0.0 224.0 jit_solution(3601049841131053343)
XLA Ops:
  0.0 1.3 collective-permute-start
  1.3 1.1 pad.15
  2.4 1.3 dynamic-slice_subtract_fusion
  3.7 1.0 collective-permute-done
  4.8 2.6 %fusion.28 = bf16[8,2,32,2056]{3,2,1,0:T(8,128)(2,1)S(1)} fusion(bf16[4,2,32,2048]{3,2,1,0:T(8,128)(2,1)S(1)} %collective-permute-done, bf16[4,2,32,2048]{3,2,1,0:T(8,128)(2,1)} %param.5), kind=kLoop, calls=%fused_computation.57 | loop fusion | flops 9474048 | bytes 4202496 | tf_op jit(solution)/shard_map/concatenate | solution.py:60
  7.3 108.7 %while.12 = (s32[]{:T(128)}, bf16[12,32,2048]{2,1,0:T(8,128)(2,1)}, f32[32,2056]{1,0:T(8,128)S(1)}, s32[12,2]{0,1:T(2,128)}, bf16[8,2,32,2056]{3,2,1,0:T(8,128)(...) while((s32[]{:T(128)}, bf16[12,32,2048]{2,1,0:T(8,128)(2,1)}, f32[32,2056]{1,0:T(8,128)S(1)}, ...), condition=%wide.region_3.4_spmd, body=%wide.region_2.3_spmd.sunk | while | flops 6569993 | bytes 17456860 | solution.py:69
  7.3 0.8 constant_dynamic-slice_fusion.2
  12.6 0.8 fusion.58
  13.5 2.2 slice_add_fusion.9
  21.7 0.8 fusion.58
  22.5 2.2 slice_add_fusion.9
  25.4 0.7 constant_dynamic-slice_fusion.2
  30.7 0.8 fusion.58
  31.6 2.2 slice_add_fusion.9
  34.5 0.7 constant_dynamic-slice_fusion.2
  39.8 0.8 fusion.58
  40.6 2.2 slice_add_fusion.9
  48.9 0.8 fusion.58
  49.7 2.2 slice_add_fusion.9
  52.6 0.7 constant_dynamic-slice_fusion.2
  57.9 0.8 fusion.58
  58.7 2.2 slice_add_fusion.9
  61.7 0.7 constant_dynamic-slice_fusion.2
  67.0 0.8 fusion.58
  67.8 2.2 slice_add_fusion.9
  76.0 0.8 fusion.58
  76.8 2.2 slice_add_fusion.9
  85.1 0.8 fusion.58
  85.9 2.2 slice_add_fusion.9
  88.8 0.7 constant_dynamic-slice_fusion.2
  94.1 0.8 fusion.58
  95.0 2.2 slice_add_fusion.9
  97.9 0.7 constant_dynamic-slice_fusion.2
  103.2 0.8 fusion.58
  104.0 2.2 slice_add_fusion.9
  106.9 0.7 constant_dynamic-slice_fusion.2
  112.3 0.8 fusion.58
  113.1 2.2 slice_add_fusion.9
  116.0 1.8 copy.210
  117.8 3.6 %fusion.48 = (bf16[12,32,1,128]{3,2,1,0:T(2,128)(2,1)S(1)}, bf16[12,32,1,128]{3,2,1,0:T(2,128)(2,1)S(1)}, bf16[12,32,1,128]{3,2,1,0:T(2,128)(2,1)S(1)}, bf16[12,...) fusion(bf16[12,32,16,128]{3,2,1,0:T(8,128)(2,1)S(1)} %bitcast.107), kind=kLoop, calls=%fused_computation.111 | loop fusion | bytes 3145728 | tf_op jit(solution)/shard_map/split | solution.py:72
  131.8 18.4 %all-to-all-start = ((bf16[16,12,32,1,128]{4,2,1,3,0:T(8,128)(2,1)}), bf16[16,12,32,1,128]{4,2,1,3,0:T(8,128)(2,1)S(1)}, u32[]{:S(2)}, u32[]{:S(2)}) async-start(bf16[16,12,32,1,128]{4,2,1,3,0:T(8,128)(2,1)} %bitcast_dynamic-update-slice_fusion), calls=%async_computation | async-start | bytes 3145728 | tf_op jit(solution)/shard_map/all_to_all | solution.py:72
  150.5 5.8 %cholesky.17 = f32[64,64]{1,0:T(8,128)S(1)} custom-call(f32[64,64]{1,0:T(8,128)S(1)} %fusion.41), custom_call_target="Cholesky" | custom-call | tf_op jit(solution)/shard_map/jit(cholesky)/cholesky | solution.py:43
  157.7 4.9 %custom-call.10 = f32[1,64,64]{1,2,0:T(8,128)S(1)} custom-call(f32[1,64,64]{2,1,0:T(8,128)S(1)} %fusion.34), custom_call_target="InvertDiagBlocksLowerTriangular" | custom-call | tf_op jit(solution)/shard_map/jit(_cho_solve)/triangular_solve | solution.py:44
  163.9 18.2 %all-to-all-done = bf16[16,12,32,1,128]{4,2,1,3,0:T(8,128)(2,1)S(1)} async-done(((bf16[16,12,32,1,128]{4,2,1,3,0:T(8,128)(2,1)}), bf16[16,12,32,1,128]{4,2,1,3,0:T(8,128)(2,1)S(1)}, u32[]{:S(2)}, u32[]{:S(2)}) %all-to-all-start) | async-done | bytes 1572896 | tf_op jit(solution)/shard_map/all_to_all | solution.py:72
  182.7 1.1 fusion.36
  183.8 1.1 fusion.46
  184.9 37.2 %all-reduce.3 = (f32[64]{0:T(128)S(1)}, f32[64]{0:T(128)S(1)}) all-reduce(f32[64]{0:T(128)S(1)} %get-tuple-element.72, f32[64]{0:T(128)S(1)} %get-tuple-element.71), channel_id=1, replica_groups=mesh['band'=2,'gx'=16] {'gx'}, use_global_device_ids=true, to_apply=%region_7.8 | all-reduce | flops 128 | bytes 1024 | tf_op jit(solution)/shard_map/psum | solution.py:92
  222.5 1.6 copy.190
  (84 shorter events, 34.8 us)
Async XLA Ops:
  0.0 4.8 %collective-permute-start = (bf16[4,2,32,2048]{3,2,1,0:T(8,128)(2,1)}, bf16[4,2,32,2048]{3,2,1,0:T(8,128)(2,1)S(1)}, u32[]{:S(2)}, u32[]{:S(2)}) collective-permute-start(bf16[4,2,32,2048]{3,2,1,0:T(8,128)(2,1)} %param.5), channel_id=1, source_target_pairs={{1,0},{2,1},{3,2},{4,3},{5,4},{6,5},{7,6},{8,7},{9,8},{10,9},{11,1... | collective-permute-start | bytes 3145736 | tf_op jit(solution)/shard_map/ppermute | solution.py:12
  131.8 18.4 %copy-start = (s32[192,2]{0,1:T(2,128)S(1)}, s32[192,2]{0,1:T(2,128)}, u32[]{:S(2)}) copy-start(s32[192,2]{0,1:T(2,128)} %param.7) | copy-start | bytes 4612
  131.8 50.3 %all-to-all-start = ((bf16[16,12,32,1,128]{4,2,1,3,0:T(8,128)(2,1)}), bf16[16,12,32,1,128]{4,2,1,3,0:T(8,128)(2,1)S(1)}, u32[]{:S(2)}, u32[]{:S(2)}) async-start(bf16[16,12,32,1,128]{4,2,1,3,0:T(8,128)(2,1)} %bitcast_dynamic-update-slice_fusion), calls=%async_computation | async-start | bytes 3145728 | tf_op jit(solution)/shard_map/all_to_all | solution.py:72
